TPU v7x, 32 devices: a whole 2x2x4 slice. The times are simulated.
32 devices in a mesh: ctx: 8 (over z, y), head: 4 (over x, core).
Axes of the slice: x: 2, y: 2, z: 4, core: 2. Of those that a mesh axis runs over, the one named last changes fastest.
Arguments:
- queries: bfloat16 [2048, 6144], P(('ctx', 'head')), may hold values from -42 to 42
- key_head_columns: bfloat16 [2048, 512], P(('ctx', 'head')), may hold values from -4 to 4
- value_head_columns: bfloat16 [2048, 512], P(('ctx', 'head')), may hold values from -6 to 6
- output_gradient: bfloat16 [2048, 6144], P(('ctx', 'head')), may hold values from -6 to 6
- file_starts: int32 [5], replicated, may hold values from 0 to 1984, as said below
- file_imports: int32 [5, 4], replicated, may hold values from -1 to 4, as said below
- header_lens: int32 [5], replicated, may hold values from 16 to 64
Outputs:
- grad_queries: float32 [2048, 6144], P(('ctx', 'head'))
- key_gradient: float32 [2048, 512], P(('ctx', 'head'))
- value_gradient: float32 [2048, 512], P(('ctx', 'head'))
Inputs may be any that keep to these rules, and one draw needn't show every extreme that they name: `file_starts`: Increasing; the first is 0 and the last is 1984; each is a multiple of 64; no two lie in the same aligned block of 256 tokens; each file has 64 tokens or more. `file_imports`: each row lists distinct files other than its own, then -1 in the unused places; file 0 imports nothing.
All inputs are finite; a program needn't handle non-finite values.
Results may differ from a plain program's by a relative error of at most 0.004.
Values may be sent and summed in bfloat16 or wider, within the bound.
No kernel may reach another device: no remote copies, remote signals or barrier semaphores. Data moves between devices by JAX's collectives and lax.ppermute only.
A program may use at most 64 MiB of HBM per device.

v0:
```python
import math
import jax
import jax.numpy as jnp
from jax import lax
from jax.sharding import PartitionSpec as P

WIN = 1024
HDR = 64


def passed_along(value, axis, steps):
    count = lax.axis_size(axis)
    first, last = (max(0, -steps), min(count, count - steps))
    return lax.ppermute(value, axis, [(source, source + steps) for source in range(first, last)])


def local_files(file_starts, file_imports, header_lens, offset_base, span_rows):
    places = offset_base + jnp.arange(span_rows, dtype=jnp.int32)
    before = file_starts[None, :] <= places[:, None]
    file_of = jnp.sum(before.astype(jnp.int32), axis=1) - 1
    file_begin = jnp.max(jnp.where(before, file_starts[None, :], 0), axis=1)
    lower_file = file_of[0]
    upper_file = file_of[span_rows - 1]
    per_file = file_imports.shape[1]
    lower_list = lax.dynamic_slice_in_dim(file_imports, lower_file, 1, 0)[0]
    upper_list = lax.dynamic_slice_in_dim(file_imports, upper_file, 1, 0)[0]
    targets = jnp.concatenate([lower_list, upper_list])
    source_file = jnp.concatenate(
        [jnp.full((per_file,), lower_file, jnp.int32), jnp.full((per_file,), upper_file, jnp.int32)]
    )
    usable = (targets >= 0) & (
        (jnp.arange(2 * per_file, dtype=jnp.int32) < per_file) | (upper_file != lower_file)
    )
    matches = jnp.arange(file_starts.shape[0], dtype=jnp.int32)[None, :] == targets[:, None]
    target_start = jnp.sum(jnp.where(matches, file_starts[None, :], 0), axis=1)
    target_len = jnp.sum(jnp.where(matches, header_lens[None, :], 0), axis=1)
    return (places, file_of, file_begin, source_file, usable, target_start, target_len)


def visibility(places, file_of, file_begin, key_places, source_file, usable, target_len):
    window_ok = (
        (key_places[None, :] <= places[:, None])
        & (key_places[None, :] > places[:, None] - WIN)
        & (key_places[None, :] >= file_begin[:, None])
    )
    offsets = jnp.arange(usable.shape[0] * HDR, dtype=jnp.int32) % HDR
    header_ok = jnp.repeat(usable, HDR) & (offsets < jnp.repeat(target_len, HDR))
    header_vis = header_ok[None, :] & (file_of[:, None] == jnp.repeat(source_file, HDR)[None, :])
    return jnp.concatenate([window_ok, header_vis], axis=1)


def per_device(
    queries,
    key_head_columns,
    value_head_columns,
    output_gradient,
    file_starts,
    file_imports,
    header_lens,
):
    query_rows, key_rows, value_rows, grad_rows = (
        lax.all_to_all(queries, "head", split_axis=1, concat_axis=0, tiled=True),
        lax.all_to_all(key_head_columns, "head", split_axis=1, concat_axis=0, tiled=True),
        lax.all_to_all(value_head_columns, "head", split_axis=1, concat_axis=0, tiled=True),
        lax.all_to_all(output_gradient, "head", split_axis=1, concat_axis=0, tiled=True),
    )
    tokens_here = key_rows.shape[0]
    head_size = key_rows.shape[1]
    queries_per_group = query_rows.shape[1] // head_size
    shard_index = lax.axis_index("ctx")
    offset_base = shard_index * tokens_here
    scaling = 1.0 / math.sqrt(head_size)
    reach = WIN // tokens_here
    places, file_of, file_begin, source_file, usable, target_start, target_len = local_files(
        file_starts, file_imports, header_lens, offset_base, tokens_here
    )
    block_count = source_file.shape[0]
    stacked = jnp.concatenate([key_rows, value_rows], axis=1)
    earlier = []
    for distance in range(1, reach + 1):
        earlier.append(passed_along(stacked, "ctx", distance))
    inside = (file_starts >= offset_base) & (file_starts < offset_base + tokens_here)
    own_offset = jnp.sum(jnp.where(inside, file_starts - offset_base, 0))
    own_header = lax.dynamic_slice_in_dim(stacked, own_offset, HDR, 0)
    all_headers = lax.all_gather(own_header, "ctx", axis=0, tiled=True)
    header_rows = jnp.concatenate(
        [
            lax.dynamic_slice_in_dim(all_headers, target_start[index] // tokens_here * HDR, HDR, 0)
            for index in range(block_count)
        ],
        axis=0,
    )
    key_table = jnp.concatenate(earlier[::-1] + [stacked, header_rows], axis=0)
    key_matrix = key_table[:, :head_size]
    value_matrix = key_table[:, head_size:]
    window_len = (reach + 1) * tokens_here
    key_places = offset_base - reach * tokens_here + jnp.arange(window_len, dtype=jnp.int32)
    visible = visibility(places, file_of, file_begin, key_places, source_file, usable, target_len)
    heads_block = max(
        (
            divisor
            for divisor in range(1, queries_per_group + 1)
            if queries_per_group % divisor == 0 and divisor * tokens_here <= max(512, tokens_here)
        )
    )
    block_total = queries_per_group // heads_block
    query_blocks = (
        query_rows.reshape(tokens_here, queries_per_group, head_size)
        .transpose(1, 0, 2)
        .reshape(block_total, heads_block, tokens_here, head_size)
    )
    grad_blocks = (
        grad_rows.reshape(tokens_here, queries_per_group, head_size)
        .transpose(1, 0, 2)
        .reshape(block_total, heads_block, tokens_here, head_size)
    )

    def attend(carry, inputs):
        key_gradient_sum, value_gradient_sum = carry
        query_block, grad_block = inputs
        scores = (
            jnp.einsum("htd,kd->htk", query_block, key_matrix, preferred_element_type=jnp.float32)
            * scaling
        )
        scores = jnp.where(visible[None], scores, -jnp.inf)
        ceiling = jnp.max(scores, axis=-1, keepdims=True)
        log_total = ceiling + jnp.log(jnp.sum(jnp.exp(scores - ceiling), axis=-1, keepdims=True))
        weights = jnp.exp(scores - log_total)
        grad_weights = jnp.einsum(
            "htd,kd->htk", grad_block, value_matrix, preferred_element_type=jnp.float32
        )
        centre = jnp.sum(weights * grad_weights, axis=-1, keepdims=True)
        grad_scores = (weights * (grad_weights - centre)).astype(jnp.bfloat16)
        weights_low = weights.astype(jnp.bfloat16)
        grad_query = (
            jnp.einsum("htk,kd->htd", grad_scores, key_matrix, preferred_element_type=jnp.float32)
            * scaling
        )
        key_gradient_sum = (
            key_gradient_sum
            + jnp.einsum(
                "htk,htd->kd", grad_scores, query_block, preferred_element_type=jnp.float32
            )
            * scaling
        )
        value_gradient_sum = value_gradient_sum + jnp.einsum(
            "htk,htd->kd", weights_low, grad_block, preferred_element_type=jnp.float32
        )
        return ((key_gradient_sum, value_gradient_sum), grad_query)

    empty_gradient = jnp.zeros((key_table.shape[0], head_size), jnp.float32)
    (key_gradient_sum, value_gradient_sum), grad_query = lax.scan(
        attend, (empty_gradient, empty_gradient), (query_blocks, grad_blocks)
    )
    grad_query = (
        grad_query.reshape(queries_per_group, tokens_here, head_size)
        .transpose(1, 0, 2)
        .reshape(tokens_here, queries_per_group * head_size)
    )
    combined = jnp.concatenate([key_gradient_sum, value_gradient_sum], axis=1)

    def window_part(index):
        return combined[index * tokens_here : (index + 1) * tokens_here]

    collected = window_part(reach)
    for distance in range(1, reach + 1):
        collected = collected + passed_along(window_part(reach - distance), "ctx", -distance)
    header_part = combined[window_len:]
    blocks_out = header_part.reshape(block_count, HDR, 2 * head_size)
    holders = jnp.where(usable, target_start // tokens_here, -1)
    block_piece = lax.all_gather(blocks_out, "ctx", axis=0, tiled=True)
    holder_piece = lax.all_gather(holders, "ctx", axis=0, tiled=True)
    selected = (holder_piece == shard_index).astype(jnp.float32)
    arriving = jnp.einsum("m,mrc->rc", selected, block_piece)
    current = lax.dynamic_slice_in_dim(collected, own_offset, HDR, 0)
    collected = lax.dynamic_update_slice_in_dim(collected, current + arriving, own_offset, 0)
    grad_queries, key_gradient, value_gradient = (
        lax.all_to_all(grad_query, "head", split_axis=0, concat_axis=1, tiled=True),
        lax.all_to_all(collected[:, :head_size], "head", split_axis=0, concat_axis=1, tiled=True),
        lax.all_to_all(collected[:, head_size:], "head", split_axis=0, concat_axis=1, tiled=True),
    )
    return (grad_queries, key_gradient, value_gradient)


def solution(mesh):
    in_specs = (
        P(("ctx", "head"), None),
        P(("ctx", "head"), None),
        P(("ctx", "head"), None),
        P(("ctx", "head"), None),
        P(),
        P(),
        P(),
    )
    out_specs = (P(("ctx", "head"), None), P(("ctx", "head"), None), P(("ctx", "head"), None))
    return jax.shard_map(
        per_device, mesh=mesh, in_specs=in_specs, out_specs=out_specs, check_vma=False
    )
```

profile of v0, /device:TPU:0, one launch (start us, length us, event | category | flops | bytes accessed | tf_op | source)
XLA Modules:
  0.0 296.5 jit_solution(10358402667834652991)
XLA Ops:
  8.7 4.2 %all-to-all-start.1 = ((bf16[64,4,128]{2,0,1:T(8,128)(2,1)}), bf16[64,4,128]{2,0,1:T(8,128)(2,1)S(1)}, u32[]{:S(2)}, u32[]{:S(2)}) async-start(bf16[64,4,128]{2,0,1:T(8,128)(2,1)} %copy_bitcast_fusion.6), calls=%async_computation.1 | async-start | bytes 131072 | tf_op jit(solution)/shard_map/all_to_all | solution.py:63
  18.2 1.5 copy_bitcast_fusion.5
  21.1 1.0 fusion.33
  23.0 1.3 dynamic-slice
  28.4 3.3 %all-to-all-start.2 = ((bf16[64,4,128]{2,0,1:T(8,128)(2,1)}), bf16[64,4,128]{2,0,1:T(8,128)(2,1)S(1)}, u32[]{:S(2)}, u32[]{:S(2)}) async-start(bf16[64,4,128]{2,0,1:T(8,128)(2,1)} %copy_bitcast_fusion.5), calls=%async_computation.2 | async-start | bytes 131072 | tf_op jit(solution)/shard_map/all_to_all | solution.py:64
  31.7 1.4 fusion.41
  55.0 1.0 copy.95
  55.9 1.0 copy.96
  57.7 3.5 %all-to-all-start.3 = ((bf16[64,4,1536]{2,0,1:T(8,128)(2,1)}), bf16[64,4,1536]{2,0,1:T(8,128)(2,1)S(1)}, u32[]{:S(2)}, u32[]{:S(2)}) async-start(bf16[64,4,1536]{2,0,1:T(8,128)(2,1)} %bitcast.142), calls=%async_computation.3 | async-start | bytes 1572864 | tf_op jit(solution)/shard_map/all_to_all | solution.py:65
  61.2 5.0 %collective-permute-start = (bf16[256,256]{1,0:T(8,128)(2,1)S(1)}, bf16[256,256]{1,0:T(8,128)(2,1)S(1)}, u32[]{:S(2)}, u32[]{:S(2)}) collective-permute-start(bf16[256,256]{1,0:T(8,128)(2,1)S(1)} %pad_maximum_fusion), channel_id=1, source_target_pairs={{0,16},{4,20},{8,24},{12,28},{1,17},{5,21},{9,25},{13,29},{2,18},{... | collective-permute-start | bytes 393224 | tf_op jit(solution)/shard_map/ppermute | solution.py:14
  66.2 4.4 %collective-permute-start.1 = (bf16[256,256]{1,0:T(8,128)(2,1)S(1)}, bf16[256,256]{1,0:T(8,128)(2,1)S(1)}, u32[]{:S(2)}, u32[]{:S(2)}) collective-permute-start(bf16[256,256]{1,0:T(8,128)(2,1)S(1)} %pad_maximum_fusion), channel_id=1, source_target_pairs={{0,12},{4,16},{8,20},{12,24},{16,28},{1,13},{5,17},{9,21},{13,25},... | collective-permute-start | bytes 393224 | tf_op jit(solution)/shard_map/ppermute | solution.py:14
  70.7 1.3 collective-permute-start.2
  72.0 3.1 %collective-permute-start.3 = (bf16[256,256]{1,0:T(8,128)(2,1)S(1)}, bf16[256,256]{1,0:T(8,128)(2,1)S(1)}, u32[]{:S(2)}, u32[]{:S(2)}) collective-permute-start(bf16[256,256]{1,0:T(8,128)(2,1)S(1)} %pad_maximum_fusion), channel_id=1, source_target_pairs={{0,4},{4,8},{8,12},{12,16},{16,20},{20,24},{24,28},{1,5},{5,9},{9,... | collective-permute-start | bytes 393224 | tf_op jit(solution)/shard_map/ppermute | solution.py:14
  75.1 31.9 %all_gather.9 = bf16[512,256]{1,0:T(8,128)(2,1)S(1)} all-gather(bf16[64,256]{1,0:T(8,128)(2,1)S(1)} %fusion.29), channel_id=1, replica_groups=mesh['ctx'=8,'head'=4] {'ctx'}, dimensions={0}, use_global_device_ids=true | all-gather | bytes 294912 | tf_op jit(solution)/shard_map/all_gather | solution.py:85
  114.7 4.2 %all-to-all-start = ((bf16[64,4,1536]{2,0,1:T(8,128)(2,1)}), bf16[64,4,1536]{2,0,1:T(8,128)(2,1)}, u32[]{:S(2)}, u32[]{:S(2)}) async-start(bf16[64,4,1536]{2,0,1:T(8,128)(2,1)} %bitcast.141), calls=%async_computation | async-start | bytes 1572864 | tf_op jit(solution)/shard_map/all_to_all | solution.py:62
  119.5 1.2 fusion.45
  120.8 1.5 reshape.109
  122.3 1.4 copy.68
  123.7 6.8 %all-to-all-done = bf16[64,4,1536]{2,0,1:T(8,128)(2,1)} async-done(((bf16[64,4,1536]{2,0,1:T(8,128)(2,1)}), bf16[64,4,1536]{2,0,1:T(8,128)(2,1)}, u32[]{:S(2)}, u32[]{:S(2)}) %all-to-all-start) | async-done | bytes 786464 | tf_op jit(solution)/shard_map/all_to_all | solution.py:62
  130.6 2.4 reshape.107
  133.0 2.3 copy.64
  135.3 68.0 %while.15 = (s32[]{:T(128)}, f32[1792,128]{1,0:T(8,128)S(1)}, f32[1792,128]{1,0:T(8,128)}, f32[6,2,256,128]{3,2,1,0:T(8,128)}, pred[256,1792]{1,0:T(8,128)(4,1)S...) while((s32[]{:T(128)}, f32[1792,128]{1,0:T(8,128)S(1)}, ...), condition=%wide.region_9.10_spmd.clone, body=%wide.region_5.9_spmd.clone.sunk | while | flops 1188461568 | bytes 80503144 | solution.py:152
  135.3 2.0 fusion.71
  137.9 1.0 multiply_reduce_fusion.2
  139.9 1.4 fusion.74
  141.2 2.1 fusion.72
  143.4 2.9 fusion.73
  146.3 2.0 fusion.71
  150.9 1.4 fusion.74
  152.3 2.1 fusion.72
  154.4 3.3 %fusion.73 = f32[1792,128]{1,0:T(8,128)} fusion(f32[2,256,1792]{2,1,0:T(8,128)S(1)} %copy-done.2, f32[2,256]{1,0:T(2,128)S(1)} %log_add_fusion.2, f32[1792,128]{1,0:T(8,128)} %get-tuple-element.220, pred[]{:T(512)S(6)} %compare.23, bf16[6,2,256,128]{3,2,1,0:T(8,128)(2,1)} %copy-done.8, s32[]{:T(128)} %get-tuple-element.218), kind=kOutput, calls=%fused_computation.10.clone.1 | convolution fusion | flops 237174784 | bytes 5638657 | tf_op jit(solution)/shard_map/while/body/eval_jaxpr/htk,htd->kd/dot_general | solution.py:146
  157.7 2.0 fusion.71
  162.3 1.4 fusion.74
  163.7 2.1 fusion.72
  165.8 3.3 %fusion.73 = f32[1792,128]{1,0:T(8,128)} fusion(f32[2,256,1792]{2,1,0:T(8,128)S(1)} %copy-done.2, f32[2,256]{1,0:T(2,128)S(1)} %log_add_fusion.2, f32[1792,128]{1,0:T(8,128)} %get-tuple-element.220, pred[]{:T(512)S(6)} %compare.23, bf16[6,2,256,128]{3,2,1,0:T(8,128)(2,1)} %copy-done.8, s32[]{:T(128)} %get-tuple-element.218), kind=kOutput, calls=%fused_computation.10.clone.1 | convolution fusion | flops 237174784 | bytes 5638657 | tf_op jit(solution)/shard_map/while/body/eval_jaxpr/htk,htd->kd/dot_general | solution.py:146
  169.1 2.0 fusion.71
  173.7 1.4 fusion.74
  175.1 2.1 fusion.72
  177.2 3.3 %fusion.73 = f32[1792,128]{1,0:T(8,128)} fusion(f32[2,256,1792]{2,1,0:T(8,128)S(1)} %copy-done.2, f32[2,256]{1,0:T(2,128)S(1)} %log_add_fusion.2, f32[1792,128]{1,0:T(8,128)} %get-tuple-element.220, pred[]{:T(512)S(6)} %compare.23, bf16[6,2,256,128]{3,2,1,0:T(8,128)(2,1)} %copy-done.8, s32[]{:T(128)} %get-tuple-element.218), kind=kOutput, calls=%fused_computation.10.clone.1 | convolution fusion | flops 237174784 | bytes 5638657 | tf_op jit(solution)/shard_map/while/body/eval_jaxpr/htk,htd->kd/dot_general | solution.py:146
  180.5 2.0 fusion.71
  185.1 1.4 fusion.74
  186.5 2.1 fusion.72
  188.6 3.3 %fusion.73 = f32[1792,128]{1,0:T(8,128)} fusion(f32[2,256,1792]{2,1,0:T(8,128)S(1)} %copy-done.2, f32[2,256]{1,0:T(2,128)S(1)} %log_add_fusion.2, f32[1792,128]{1,0:T(8,128)} %get-tuple-element.220, pred[]{:T(512)S(6)} %compare.23, bf16[6,2,256,128]{3,2,1,0:T(8,128)(2,1)} %copy-done.8, s32[]{:T(128)} %get-tuple-element.218), kind=kOutput, calls=%fused_computation.10.clone.1 | convolution fusion | flops 237174784 | bytes 5638657 | tf_op jit(solution)/shard_map/while/body/eval_jaxpr/htk,htd->kd/dot_general | solution.py:146
  191.9 2.0 fusion.71
  196.5 1.4 fusion.74
  197.9 2.1 fusion.72
  200.0 3.3 %fusion.73 = f32[1792,128]{1,0:T(8,128)} fusion(f32[2,256,1792]{2,1,0:T(8,128)S(1)} %copy-done.2, f32[2,256]{1,0:T(2,128)S(1)} %log_add_fusion.2, f32[1792,128]{1,0:T(8,128)} %get-tuple-element.220, pred[]{:T(512)S(6)} %compare.23, bf16[6,2,256,128]{3,2,1,0:T(8,128)(2,1)} %copy-done.8, s32[]{:T(128)} %get-tuple-element.218), kind=kOutput, calls=%fused_computation.10.clone.1 | convolution fusion | flops 237174784 | bytes 5638657 | tf_op jit(solution)/shard_map/while/body/eval_jaxpr/htk,htd->kd/dot_general | solution.py:146
  203.4 1.1 copy-done.3
  205.4 1.1 fusion.44
  206.4 1.3 collective-permute-start.4
  207.7 1.3 collective-permute-start.5
  209.0 1.3 collective-permute-start.6
  210.3 1.5 collective-permute-start.7
  211.8 2.4 copy.94
  214.2 1.4 all_to_all.108
  215.5 3.6 %all-to-all-start.4 = ((f32[4,64,1536]{2,1,0:T(8,128)}), f32[4,64,1536]{2,1,0:T(8,128)S(1)}, u32[]{:S(2)}, u32[]{:S(2)}) async-start(f32[4,64,1536]{2,1,0:T(8,128)} %all_to_all.108), calls=%async_computation.4 | async-start | bytes 3145728 | tf_op jit(solution)/shard_map/all_to_all | solution.py:178
  219.1 48.7 %all-reduce.1 = s32[64]{0:T(128)S(1)} all-reduce(s32[64]{0:T(128)S(1)} %get-tuple-element.118), channel_id=1, replica_groups=mesh['ctx'=8,'head'=4] {'ctx'}, use_global_device_ids=true, to_apply=%add.1 | all-reduce | flops 64 | bytes 512
  267.8 1.2 fusion.28
  269.1 2.8 fusion.24
  273.2 3.3 %all-to-all-start.6 = ((f32[4,64,128]{2,1,0:T(8,128)}), f32[4,64,128]{2,1,0:T(8,128)S(1)}, u32[]{:S(2)}, u32[]{:S(2)}) async-start(f32[4,64,128]{2,1,0:T(8,128)} %bitcast.29), calls=%async_computation.6 | async-start | bytes 262144 | tf_op jit(solution)/shard_map/all_to_all | solution.py:180
  276.5 1.3 copy.81
  277.8 3.3 %all-to-all-done.6 = f32[4,64,128]{2,1,0:T(8,128)S(1)} async-done(((f32[4,64,128]{2,1,0:T(8,128)}), f32[4,64,128]{2,1,0:T(8,128)S(1)}, u32[]{:S(2)}, u32[]{:S(2)}) %all-to-all-start.6) | async-done | bytes 131104 | tf_op jit(solution)/shard_map/all_to_all | solution.py:180
  281.1 3.3 %all-to-all-start.5 = ((f32[4,64,128]{2,1,0:T(8,128)}), f32[4,64,128]{2,1,0:T(8,128)S(1)}, u32[]{:S(2)}, u32[]{:S(2)}) async-start(f32[4,64,128]{2,1,0:T(8,128)} %bitcast.27), calls=%async_computation.5 | async-start | bytes 262144 | tf_op jit(solution)/shard_map/all_to_all | solution.py:179
  285.1 3.9 %all-to-all-done.5 = f32[4,64,128]{2,1,0:T(8,128)S(1)} async-done(((f32[4,64,128]{2,1,0:T(8,128)}), f32[4,64,128]{2,1,0:T(8,128)S(1)}, u32[]{:S(2)}, u32[]{:S(2)}) %all-to-all-start.5) | async-done | bytes 131104 | tf_op jit(solution)/shard_map/all_to_all | solution.py:179
  (192 shorter events, 33.7 us)
Async XLA Ops:
  7.2 47.8 %copy-start.11 = (bf16[64,6144]{1,0:T(8,128)(2,1)S(1)}, bf16[64,6144]{1,0:T(8,128)(2,1)}, u32[]{:S(2)}) copy-start(bf16[64,6144]{1,0:T(8,128)(2,1)} %param.12) | copy-start | bytes 2359300
  8.0 47.9 %copy-start.12 = (bf16[64,6144]{1,0:T(8,128)(2,1)S(1)}, bf16[64,6144]{1,0:T(8,128)(2,1)}, u32[]{:S(2)}) copy-start(bf16[64,6144]{1,0:T(8,128)(2,1)} %param.9) | copy-start | bytes 2359300
  8.7 19.7 %all-to-all-start.1 = ((bf16[64,4,128]{2,0,1:T(8,128)(2,1)}), bf16[64,4,128]{2,0,1:T(8,128)(2,1)S(1)}, u32[]{:S(2)}, u32[]{:S(2)}) async-start(bf16[64,4,128]{2,0,1:T(8,128)(2,1)} %copy_bitcast_fusion.6), calls=%async_computation.1 | async-start | bytes 131072 | tf_op jit(solution)/shard_map/all_to_all | solution.py:63
  28.4 29.3 %all-to-all-start.2 = ((bf16[64,4,128]{2,0,1:T(8,128)(2,1)}), bf16[64,4,128]{2,0,1:T(8,128)(2,1)S(1)}, u32[]{:S(2)}, u32[]{:S(2)}) async-start(bf16[64,4,128]{2,0,1:T(8,128)(2,1)} %copy_bitcast_fusion.5), calls=%async_computation.2 | async-start | bytes 131072 | tf_op jit(solution)/shard_map/all_to_all | solution.py:64
  57.7 57.0 %all-to-all-start.3 = ((bf16[64,4,1536]{2,0,1:T(8,128)(2,1)}), bf16[64,4,1536]{2,0,1:T(8,128)(2,1)S(1)}, u32[]{:S(2)}, u32[]{:S(2)}) async-start(bf16[64,4,1536]{2,0,1:T(8,128)(2,1)} %bitcast.142), calls=%async_computation.3 | async-start | bytes 1572864 | tf_op jit(solution)/shard_map/all_to_all | solution.py:65
  61.2 45.8 %collective-permute-start = (bf16[256,256]{1,0:T(8,128)(2,1)S(1)}, bf16[256,256]{1,0:T(8,128)(2,1)S(1)}, u32[]{:S(2)}, u32[]{:S(2)}) collective-permute-start(bf16[256,256]{1,0:T(8,128)(2,1)S(1)} %pad_maximum_fusion), channel_id=1, source_target_pairs={{0,16},{4,20},{8,24},{12,28},{1,17},{5,21},{9,25},{13,29},{2,18},{... | collective-permute-start | bytes 393224 | tf_op jit(solution)/shard_map/ppermute | solution.py:14
  66.2 41.5 %collective-permute-start.1 = (bf16[256,256]{1,0:T(8,128)(2,1)S(1)}, bf16[256,256]{1,0:T(8,128)(2,1)S(1)}, u32[]{:S(2)}, u32[]{:S(2)}) collective-permute-start(bf16[256,256]{1,0:T(8,128)(2,1)S(1)} %pad_maximum_fusion), channel_id=1, source_target_pairs={{0,12},{4,16},{8,20},{12,24},{16,28},{1,13},{5,17},{9,21},{13,25},... | collective-permute-start | bytes 393224 | tf_op jit(solution)/shard_map/ppermute | solution.py:14
  70.7 37.7 %collective-permute-start.2 = (bf16[256,256]{1,0:T(8,128)(2,1)S(1)}, bf16[256,256]{1,0:T(8,128)(2,1)S(1)}, u32[]{:S(2)}, u32[]{:S(2)}) collective-permute-start(bf16[256,256]{1,0:T(8,128)(2,1)S(1)} %pad_maximum_fusion), channel_id=1, source_target_pairs={{0,8},{4,12},{8,16},{12,20},{16,24},{20,28},{1,9},{5,13},{9,17},{1... | collective-permute-start | bytes 393224 | tf_op jit(solution)/shard_map/ppermute | solution.py:14
  72.0 37.0 %collective-permute-start.3 = (bf16[256,256]{1,0:T(8,128)(2,1)S(1)}, bf16[256,256]{1,0:T(8,128)(2,1)S(1)}, u32[]{:S(2)}, u32[]{:S(2)}) collective-permute-start(bf16[256,256]{1,0:T(8,128)(2,1)S(1)} %pad_maximum_fusion), channel_id=1, source_target_pairs={{0,4},{4,8},{8,12},{12,16},{16,20},{20,24},{24,28},{1,5},{5,9},{9,... | collective-permute-start | bytes 393224 | tf_op jit(solution)/shard_map/ppermute | solution.py:14
  114.7 15.9 %all-to-all-start = ((bf16[64,4,1536]{2,0,1:T(8,128)(2,1)}), bf16[64,4,1536]{2,0,1:T(8,128)(2,1)}, u32[]{:S(2)}, u32[]{:S(2)}) async-start(bf16[64,4,1536]{2,0,1:T(8,128)(2,1)} %bitcast.141), calls=%async_computation | async-start | bytes 1572864 | tf_op jit(solution)/shard_map/all_to_all | solution.py:62
  118.9 150.2 %all-gather.2.cloned.1.call-start = ((), (), s32[]{:S(2)}) async-start(), calls=%async_computation.7 | async-start | bytes 2359296 | tf_op jit(solution)/shard_map/all_gather | solution.py:171
  135.3 2.0 copy-start.4
  135.3 2.6 copy-start.6
  135.3 3.6 %copy-start.8 = (bf16[6,2,256,128]{3,2,1,0:T(8,128)(2,1)}, bf16[6,2,256,128]{3,2,1,0:T(8,128)(2,1)S(1)}, u32[]{:S(2)}) copy-start(bf16[6,2,256,128]{3,2,1,0:T(8,128)(2,1)S(1)} %get-tuple-element.236) | copy-start | bytes 2359300 | tf_op jit(solution)/shard_map/while
  137.3 1.8 copy-start.1
  141.2 2.1 copy-start.2
  143.3 3.0 %copy-start.5 = (pred[256,1792]{1,0:T(8,128)(4,1)S(1)}, pred[256,1792]{1,0:T(8,128)(4,1)}, u32[]{:S(2)}) copy-start(pred[256,1792]{1,0:T(8,128)(4,1)} %copy-done.4) | copy-start | bytes 1376260 | tf_op jit(solution)/shard_map/while
  143.3 3.0 %copy-start.7 = (bf16[1792,128]{1,0:T(8,128)(2,1)S(1)}, bf16[1792,128]{1,0:T(8,128)(2,1)}, u32[]{:S(2)}) copy-start(bf16[1792,128]{1,0:T(8,128)(2,1)} %copy-done.6) | copy-start | bytes 1376260 | tf_op jit(solution)/shard_map/while
  143.3 3.0 copy-start.9
  146.3 2.0 copy-start.4
  146.3 2.7 copy-start.6
  146.3 3.6 %copy-start.8 = (bf16[6,2,256,128]{3,2,1,0:T(8,128)(2,1)}, bf16[6,2,256,128]{3,2,1,0:T(8,128)(2,1)S(1)}, u32[]{:S(2)}) copy-start(bf16[6,2,256,128]{3,2,1,0:T(8,128)(2,1)S(1)} %get-tuple-element.236) | copy-start | bytes 2359300 | tf_op jit(solution)/shard_map/while
  148.3 1.8 copy-start.1
  152.3 2.1 copy-start.2
  154.4 3.3 %copy-start.5 = (pred[256,1792]{1,0:T(8,128)(4,1)S(1)}, pred[256,1792]{1,0:T(8,128)(4,1)}, u32[]{:S(2)}) copy-start(pred[256,1792]{1,0:T(8,128)(4,1)} %copy-done.4) | copy-start | bytes 1376260 | tf_op jit(solution)/shard_map/while
  154.4 3.3 %copy-start.7 = (bf16[1792,128]{1,0:T(8,128)(2,1)S(1)}, bf16[1792,128]{1,0:T(8,128)(2,1)}, u32[]{:S(2)}) copy-start(bf16[1792,128]{1,0:T(8,128)(2,1)} %copy-done.6) | copy-start | bytes 1376260 | tf_op jit(solution)/shard_map/while
  154.4 3.3 %copy-start.9 = (bf16[6,2,256,128]{3,2,1,0:T(8,128)(2,1)S(1)}, bf16[6,2,256,128]{3,2,1,0:T(8,128)(2,1)}, u32[]{:S(2)}) copy-start(bf16[6,2,256,128]{3,2,1,0:T(8,128)(2,1)} %copy-done.8) | copy-start | bytes 2359300 | tf_op jit(solution)/shard_map/while
  157.7 2.0 copy-start.4
  157.7 2.7 copy-start.6
  157.7 3.6 %copy-start.8 = (bf16[6,2,256,128]{3,2,1,0:T(8,128)(2,1)}, bf16[6,2,256,128]{3,2,1,0:T(8,128)(2,1)S(1)}, u32[]{:S(2)}) copy-start(bf16[6,2,256,128]{3,2,1,0:T(8,128)(2,1)S(1)} %get-tuple-element.236) | copy-start | bytes 2359300 | tf_op jit(solution)/shard_map/while
  159.7 1.8 copy-start.1
  163.7 2.1 copy-start.2
  165.8 3.3 %copy-start.5 = (pred[256,1792]{1,0:T(8,128)(4,1)S(1)}, pred[256,1792]{1,0:T(8,128)(4,1)}, u32[]{:S(2)}) copy-start(pred[256,1792]{1,0:T(8,128)(4,1)} %copy-done.4) | copy-start | bytes 1376260 | tf_op jit(solution)/shard_map/while
  165.8 3.3 %copy-start.7 = (bf16[1792,128]{1,0:T(8,128)(2,1)S(1)}, bf16[1792,128]{1,0:T(8,128)(2,1)}, u32[]{:S(2)}) copy-start(bf16[1792,128]{1,0:T(8,128)(2,1)} %copy-done.6) | copy-start | bytes 1376260 | tf_op jit(solution)/shard_map/while
  165.8 3.3 %copy-start.9 = (bf16[6,2,256,128]{3,2,1,0:T(8,128)(2,1)S(1)}, bf16[6,2,256,128]{3,2,1,0:T(8,128)(2,1)}, u32[]{:S(2)}) copy-start(bf16[6,2,256,128]{3,2,1,0:T(8,128)(2,1)} %copy-done.8) | copy-start | bytes 2359300 | tf_op jit(solution)/shard_map/while
  169.1 2.0 copy-start.4
  169.1 2.7 copy-start.6
  169.1 3.6 %copy-start.8 = (bf16[6,2,256,128]{3,2,1,0:T(8,128)(2,1)}, bf16[6,2,256,128]{3,2,1,0:T(8,128)(2,1)S(1)}, u32[]{:S(2)}) copy-start(bf16[6,2,256,128]{3,2,1,0:T(8,128)(2,1)S(1)} %get-tuple-element.236) | copy-start | bytes 2359300 | tf_op jit(solution)/shard_map/while
  175.1 2.1 copy-start.2
  177.2 3.3 %copy-start.5 = (pred[256,1792]{1,0:T(8,128)(4,1)S(1)}, pred[256,1792]{1,0:T(8,128)(4,1)}, u32[]{:S(2)}) copy-start(pred[256,1792]{1,0:T(8,128)(4,1)} %copy-done.4) | copy-start | bytes 1376260 | tf_op jit(solution)/shard_map/while
  177.2 3.3 %copy-start.7 = (bf16[1792,128]{1,0:T(8,128)(2,1)S(1)}, bf16[1792,128]{1,0:T(8,128)(2,1)}, u32[]{:S(2)}) copy-start(bf16[1792,128]{1,0:T(8,128)(2,1)} %copy-done.6) | copy-start | bytes 1376260 | tf_op jit(solution)/shard_map/while
  177.2 3.3 %copy-start.9 = (bf16[6,2,256,128]{3,2,1,0:T(8,128)(2,1)S(1)}, bf16[6,2,256,128]{3,2,1,0:T(8,128)(2,1)}, u32[]{:S(2)}) copy-start(bf16[6,2,256,128]{3,2,1,0:T(8,128)(2,1)} %copy-done.8) | copy-start | bytes 2359300 | tf_op jit(solution)/shard_map/while
  180.5 2.0 copy-start.4
  180.5 2.7 copy-start.6
  180.5 3.6 %copy-start.8 = (bf16[6,2,256,128]{3,2,1,0:T(8,128)(2,1)}, bf16[6,2,256,128]{3,2,1,0:T(8,128)(2,1)S(1)}, u32[]{:S(2)}) copy-start(bf16[6,2,256,128]{3,2,1,0:T(8,128)(2,1)S(1)} %get-tuple-element.236) | copy-start | bytes 2359300 | tf_op jit(solution)/shard_map/while
  186.5 2.1 copy-start.2
  188.6 3.3 %copy-start.5 = (pred[256,1792]{1,0:T(8,128)(4,1)S(1)}, pred[256,1792]{1,0:T(8,128)(4,1)}, u32[]{:S(2)}) copy-start(pred[256,1792]{1,0:T(8,128)(4,1)} %copy-done.4) | copy-start | bytes 1376260 | tf_op jit(solution)/shard_map/while
  188.6 3.3 %copy-start.7 = (bf16[1792,128]{1,0:T(8,128)(2,1)S(1)}, bf16[1792,128]{1,0:T(8,128)(2,1)}, u32[]{:S(2)}) copy-start(bf16[1792,128]{1,0:T(8,128)(2,1)} %copy-done.6) | copy-start | bytes 1376260 | tf_op jit(solution)/shard_map/while
  188.6 3.3 %copy-start.9 = (bf16[6,2,256,128]{3,2,1,0:T(8,128)(2,1)S(1)}, bf16[6,2,256,128]{3,2,1,0:T(8,128)(2,1)}, u32[]{:S(2)}) copy-start(bf16[6,2,256,128]{3,2,1,0:T(8,128)(2,1)} %copy-done.8) | copy-start | bytes 2359300 | tf_op jit(solution)/shard_map/while
  191.9 2.0 copy-start.4
  191.9 2.7 copy-start.6
  191.9 3.6 %copy-start.8 = (bf16[6,2,256,128]{3,2,1,0:T(8,128)(2,1)}, bf16[6,2,256,128]{3,2,1,0:T(8,128)(2,1)S(1)}, u32[]{:S(2)}) copy-start(bf16[6,2,256,128]{3,2,1,0:T(8,128)(2,1)S(1)} %get-tuple-element.236) | copy-start | bytes 2359300 | tf_op jit(solution)/shard_map/while
  197.9 2.1 copy-start.2
  200.0 3.3 %copy-start.5 = (pred[256,1792]{1,0:T(8,128)(4,1)S(1)}, pred[256,1792]{1,0:T(8,128)(4,1)}, u32[]{:S(2)}) copy-start(pred[256,1792]{1,0:T(8,128)(4,1)} %copy-done.4) | copy-start | bytes 1376260 | tf_op jit(solution)/shard_map/while
  200.0 3.3 %copy-start.7 = (bf16[1792,128]{1,0:T(8,128)(2,1)S(1)}, bf16[1792,128]{1,0:T(8,128)(2,1)}, u32[]{:S(2)}) copy-start(bf16[1792,128]{1,0:T(8,128)(2,1)} %copy-done.6) | copy-start | bytes 1376260 | tf_op jit(solution)/shard_map/while
  200.0 3.3 %copy-start.9 = (bf16[6,2,256,128]{3,2,1,0:T(8,128)(2,1)S(1)}, bf16[6,2,256,128]{3,2,1,0:T(8,128)(2,1)}, u32[]{:S(2)}) copy-start(bf16[6,2,256,128]{3,2,1,0:T(8,128)(2,1)} %copy-done.8) | copy-start | bytes 2359300 | tf_op jit(solution)/shard_map/while
  204.5 7.3 %copy-start.10 = (f32[1792,256]{1,0:T(8,128)}, f32[1792,256]{1,0:T(8,128)S(1)}, u32[]{:S(2)}) copy-start(f32[1792,256]{1,0:T(8,128)S(1)} %constant_dynamic-update-slice_fusion.13) | copy-start | bytes 5505028
  206.4 61.4 %collective-permute-start.4 = (f32[256,256]{1,0:T(8,128)}, f32[256,256]{1,0:T(8,128)S(1)}, u32[]{:S(2)}, u32[]{:S(2)}) collective-permute-start(f32[256,256]{1,0:T(8,128)} %get-tuple-element.124), channel_id=1, source_target_pairs={{4,0},{8,4},{12,8},{16,12},{20,16},{24,20},{28,24},{5,1},{9,5},{13... | collective-permute-start | bytes 786440 | tf_op jit(solution)/shard_map/ppermute | solution.py:14
  207.7 60.1 %collective-permute-start.5 = (f32[256,256]{1,0:T(8,128)}, f32[256,256]{1,0:T(8,128)S(1)}, u32[]{:S(2)}, u32[]{:S(2)}) collective-permute-start(f32[256,256]{1,0:T(8,128)} %get-tuple-element.127), channel_id=1, source_target_pairs={{8,0},{12,4},{16,8},{20,12},{24,16},{28,20},{9,1},{13,5},{17,9},{2... | collective-permute-start | bytes 786440 | tf_op jit(solution)/shard_map/ppermute | solution.py:14
  209.0 58.8 %collective-permute-start.6 = (f32[256,256]{1,0:T(8,128)}, f32[256,256]{1,0:T(8,128)}, u32[]{:S(2)}, u32[]{:S(2)}) collective-permute-start(f32[256,256]{1,0:T(8,128)} %get-tuple-element.126), channel_id=1, source_target_pairs={{12,0},{16,4},{20,8},{24,12},{28,16},{13,1},{17,5},{21,9},{25,13},... | collective-permute-start | bytes 786440 | tf_op jit(solution)/shard_map/ppermute | solution.py:14
  210.3 57.5 %collective-permute-start.7 = (f32[256,256]{1,0:T(8,128)}, f32[256,256]{1,0:T(8,128)}, u32[]{:S(2)}, u32[]{:S(2)}) collective-permute-start(f32[256,256]{1,0:T(8,128)} %get-tuple-element.125), channel_id=1, source_target_pairs={{16,0},{20,4},{24,8},{28,12},{17,1},{21,5},{25,9},{29,13},{18,2},{... | collective-permute-start | bytes 786440 | tf_op jit(solution)/shard_map/ppermute | solution.py:14
  215.5 57.6 %all-to-all-start.4 = ((f32[4,64,1536]{2,1,0:T(8,128)}), f32[4,64,1536]{2,1,0:T(8,128)S(1)}, u32[]{:S(2)}, u32[]{:S(2)}) async-start(f32[4,64,1536]{2,1,0:T(8,128)} %all_to_all.108), calls=%async_computation.4 | async-start | bytes 3145728 | tf_op jit(solution)/shard_map/all_to_all | solution.py:178
  273.2 7.9 %all-to-all-start.6 = ((f32[4,64,128]{2,1,0:T(8,128)}), f32[4,64,128]{2,1,0:T(8,128)S(1)}, u32[]{:S(2)}, u32[]{:S(2)}) async-start(f32[4,64,128]{2,1,0:T(8,128)} %bitcast.29), calls=%async_computation.6 | async-start | bytes 262144 | tf_op jit(solution)/shard_map/all_to_all | solution.py:180
  281.1 7.9 %all-to-all-start.5 = ((f32[4,64,128]{2,1,0:T(8,128)}), f32[4,64,128]{2,1,0:T(8,128)S(1)}, u32[]{:S(2)}, u32[]{:S(2)}) async-start(f32[4,64,128]{2,1,0:T(8,128)} %bitcast.27), calls=%async_computation.5 | async-start | bytes 262144 | tf_op jit(solution)/shard_map/all_to_all | solution.py:179
  (5 other events, 7.4 us)
Sparse Core Ops, SparseCore 0:
  205.5 60.7 all-gather.1
where the time goes:
time: 299 us; the launch traced here: 296 us
  blocking collectives  80.6 us (27%)
  matrix products  60.3 us (20%)
  starting transfers between devices  44.7 us (15%)
  between operations  43 us (14%)
  local copies, waits for them, and re-layouts  38.6 us (13%)
  other arithmetic  14.6 us (5%)
  waiting for transfers between devices  14.1 us (5%)
    unnamed x1, blocking collectives  48.7 us
    all_gather x1, blocking collectives, per_device(): all_headers = lax.all_gather(own_header, 'ctx', axis=0, tiled=True)  31.9 us
    dot_general x6, matrix products, attend(): jnp.einsum('htk,htd->kd', weights_low, grad_block, preferred_element_type...  19.3 us
    ppermute x8, starting transfers between devices, passed_along(): lax.ppermute(value, axis, [(source, source + steps) for source in range(f...  19.2 us
    dot_general x6, matrix products, attend(): jnp.einsum('htk,htd->kd', grad_scores, query_block, preferred_element_typ...  12.4 us
    dot_general x6, matrix products, attend(): jnp.einsum('htd,kd->htk', query_block, key_matrix, preferred_element_type...  11.8 us
    unnamed x24, local copies, waits for them, and re-layouts  10.3 us
    dot_general x6, matrix products, attend(): jnp.einsum('htk,kd->htd', grad_scores, key_matrix, preferred_element_type...  8.1 us
  transfers between devices with their start and end apart: 16, of which 3 were waited for; matrix products, arithmetic and copies ran while one was open for 12% of the time, Pallas kernels for 0%

commit v1 on v0

--- a/solution.py
+++ b/solution.py
@@ -6,6 +6,28 @@
 
 WIN = 1024
 HDR = 64
+
+
+def in_order(blocks, dim):
+    blocks = jnp.moveaxis(blocks, 0, dim)
+    dims = blocks.shape
+    return blocks.reshape(*dims[:dim], dims[dim] * dims[dim + 1], *dims[dim + 2 :])
+
+
+def ring_gather(value, axis, dim):
+    length = lax.axis_size(axis)
+    pairs = [(i, (i + 1) % length) for i in range(length)]
+    back = [(b, a) for a, b in pairs]
+    lower, upper = ([], [])
+    for step in range(length - 1):
+        if step % 2 == 0:
+            lower.append(lax.ppermute(lower[-1] if lower else value, axis, pairs))
+        else:
+            upper.append(lax.ppermute(upper[-1] if upper else value, axis, back))
+    blocks = jnp.stack([*lower[::-1], value, *upper])
+    shift = lax.axis_index(axis) - len(lower)
+    blocks = blocks[(jnp.arange(length) - shift) % length]
+    return in_order(blocks, dim)
 
 
 def passed_along(value, axis, steps):
@@ -82,7 +104,7 @@
     inside = (file_starts >= offset_base) & (file_starts < offset_base + tokens_here)
     own_offset = jnp.sum(jnp.where(inside, file_starts - offset_base, 0))
     own_header = lax.dynamic_slice_in_dim(stacked, own_offset, HDR, 0)
-    all_headers = lax.all_gather(own_header, "ctx", axis=0, tiled=True)
+    all_headers = ring_gather(own_header, "ctx", 0)
     header_rows = jnp.concatenate(
         [
             lax.dynamic_slice_in_dim(all_headers, target_start[index] // tokens_here * HDR, HDR, 0)

time: 299 us -> 286 us (0.957)
  blocking collectives: 80.6 us -> 50.2 us
  starting transfers between devices: 44.7 us -> 58.8 us
    all_gather x1 -> x0, blocking collectives: 31.9 us -> none  [per_device(): all_headers = lax.all_gather(own_header, 'ctx', axis=0, tiled=True)]
    ppermute x0 -> x7, starting transfers between devices: none -> 10.5 us  [the longest x3 5.66 us: ring_gather(): upper.append(lax.ppermute(upper[-1] if upper else value, axis, back))]
    ppermute x8, starting transfers between devices: 19.2 us -> 22.9 us  [passed_along(): lax.ppermute(value, axis, [(source, source + steps) for source in range(f...]
    unnamed x24 -> x29, local copies, waits for them, and re-layouts: 10.3 us -> 10.3 us
  transfers between devices with their start and end apart: 16 -> 23, of which waited for: 3 -> 5; matrix products, arithmetic and copies ran while one was open for 12% -> 13% of each run, Pallas kernels for 0% -> 0%
where the time goes in v1:
time: 286 us; the launch traced here: 284 us
  matrix products  60.2 us (21%)
  starting transfers between devices  58.8 us (21%)
  blocking collectives  50.2 us (18%)
  between operations  42.9 us (15%)
  local copies, waits for them, and re-layouts  40.3 us (14%)
  waiting for transfers between devices  16 us (6%)
  other arithmetic  14.5 us (5%)
    unnamed x1, blocking collectives  50.2 us
    ppermute x8, starting transfers between devices, passed_along(): lax.ppermute(value, axis, [(source, source + steps) for source in range(f...  22.9 us
    dot_general x6, matrix products, attend(): jnp.einsum('htk,htd->kd', weights_low, grad_block, preferred_element_type...  19.2 us
    dot_general x6, matrix products, attend(): jnp.einsum('htk,htd->kd', grad_scores, query_block, preferred_element_typ...  12.5 us
    dot_general x6, matrix products, attend(): jnp.einsum('htd,kd->htk', query_block, key_matrix, preferred_element_type...  11.9 us
    unnamed x29, local copies, waits for them, and re-layouts  10.3 us
    dot_general x6, matrix products, attend(): jnp.einsum('htk,kd->htd', grad_scores, key_matrix, preferred_element_type...  8.1 us
    all_to_all x1, waiting for transfers between devices, per_device(): lax.all_to_all(queries, 'head', split_axis=1, concat_axis=0, tiled=True)  6.84 us
  transfers between devices with their start and end apart: 23, of which 5 were waited for; matrix products, arithmetic and copies ran while one was open for 13% of the time, Pallas kernels for 0%

profile of v1, /device:TPU:0, one launch (start us, length us, event | category | flops | bytes accessed | tf_op | source)
XLA Modules:
  0.0 283.6 jit_solution(6338173375911563007)
XLA Ops:
  8.7 4.2 %all-to-all-start.1 = ((bf16[64,4,128]{2,0,1:T(8,128)(2,1)}), bf16[64,4,128]{2,0,1:T(8,128)(2,1)S(1)}, u32[]{:S(2)}, u32[]{:S(2)}) async-start(bf16[64,4,128]{2,0,1:T(8,128)(2,1)} %copy_bitcast_fusion.6), calls=%async_computation.1 | async-start | bytes 131072 | tf_op jit(solution)/shard_map/all_to_all | solution.py:85
  18.0 1.5 copy_bitcast_fusion.5
  22.8 1.3 dynamic-slice
  28.1 3.3 %all-to-all-start.2 = ((bf16[64,4,128]{2,0,1:T(8,128)(2,1)}), bf16[64,4,128]{2,0,1:T(8,128)(2,1)S(1)}, u32[]{:S(2)}, u32[]{:S(2)}) async-start(bf16[64,4,128]{2,0,1:T(8,128)(2,1)} %copy_bitcast_fusion.5), calls=%async_computation.2 | async-start | bytes 131072 | tf_op jit(solution)/shard_map/all_to_all | solution.py:86
  31.4 1.3 fusion.43
  35.6 3.5 %all-to-all-start.3 = ((bf16[64,4,1536]{2,0,1:T(8,128)(2,1)}), bf16[64,4,1536]{2,0,1:T(8,128)(2,1)S(1)}, u32[]{:S(2)}, u32[]{:S(2)}) async-start(bf16[64,4,1536]{2,0,1:T(8,128)(2,1)} %bitcast.127), calls=%async_computation.3 | async-start | bytes 1572864 | tf_op jit(solution)/shard_map/all_to_all | solution.py:87
  39.2 2.1 collective-permute-start.4
  41.3 3.1 %collective-permute-start.8 = (bf16[64,256]{1,0:T(8,128)(2,1)S(1)}, bf16[64,256]{1,0:T(8,128)(2,1)S(1)}, u32[]{:S(2)}, u32[]{:S(2)}) collective-permute-start(bf16[64,256]{1,0:T(8,128)(2,1)S(1)} %fusion.29), channel_id=1, source_target_pairs={{4,0},{8,4},{12,8},{16,12},{20,16},{24,20},{28,24},{0,28},{5,1},{9... | collective-permute-start | bytes 98312 | tf_op jit(solution)/shard_map/ppermute | solution.py:26
  44.4 2.8 collective-permute-start
  47.9 2.9 %collective-permute-start.1 = (bf16[256,256]{1,0:T(8,128)(2,1)S(1)}, bf16[256,256]{1,0:T(8,128)(2,1)S(1)}, u32[]{:S(2)}, u32[]{:S(2)}) collective-permute-start(bf16[256,256]{1,0:T(8,128)(2,1)S(1)} %pad_maximum_fusion), channel_id=1, source_target_pairs={{0,12},{4,16},{8,20},{12,24},{16,28},{1,13},{5,17},{9,21},{13,25},... | collective-permute-start | bytes 393224 | tf_op jit(solution)/shard_map/ppermute | solution.py:36
  50.9 2.5 collective-permute-start.9
  74.6 2.1 copy.96
  76.8 6.5 %collective-permute-start.2 = (bf16[256,256]{1,0:T(8,128)(2,1)S(1)}, bf16[256,256]{1,0:T(8,128)(2,1)S(1)}, u32[]{:S(2)}, u32[]{:S(2)}) collective-permute-start(bf16[256,256]{1,0:T(8,128)(2,1)S(1)} %pad_maximum_fusion), channel_id=1, source_target_pairs={{0,8},{4,12},{8,16},{12,20},{16,24},{20,28},{1,9},{5,13},{9,17},{1... | collective-permute-start | bytes 393224 | tf_op jit(solution)/shard_map/ppermute | solution.py:36
  83.3 5.3 %collective-permute-start.3 = (bf16[256,256]{1,0:T(8,128)(2,1)S(1)}, bf16[256,256]{1,0:T(8,128)(2,1)S(1)}, u32[]{:S(2)}, u32[]{:S(2)}) collective-permute-start(bf16[256,256]{1,0:T(8,128)(2,1)S(1)} %pad_maximum_fusion), channel_id=1, source_target_pairs={{0,4},{4,8},{8,12},{12,16},{16,20},{20,24},{24,28},{1,5},{5,9},{9,... | collective-permute-start | bytes 393224 | tf_op jit(solution)/shard_map/ppermute | solution.py:36
  88.7 2.0 collective-permute-start.7
  94.0 1.3 collective-permute-done.7
  100.3 4.2 %all-to-all-start = ((bf16[64,4,1536]{2,0,1:T(8,128)(2,1)}), bf16[64,4,1536]{2,0,1:T(8,128)(2,1)}, u32[]{:S(2)}, u32[]{:S(2)}) async-start(bf16[64,4,1536]{2,0,1:T(8,128)(2,1)} %bitcast.160), calls=%async_computation | async-start | bytes 1572864 | tf_op jit(solution)/shard_map/all_to_all | solution.py:84
  105.2 1.2 fusion.47
  106.4 1.5 reshape.162
  107.9 1.4 copy.68
  109.4 6.8 %all-to-all-done = bf16[64,4,1536]{2,0,1:T(8,128)(2,1)} async-done(((bf16[64,4,1536]{2,0,1:T(8,128)(2,1)}), bf16[64,4,1536]{2,0,1:T(8,128)(2,1)}, u32[]{:S(2)}, u32[]{:S(2)}) %all-to-all-start) | async-done | bytes 786464 | tf_op jit(solution)/shard_map/all_to_all | solution.py:84
  116.2 2.4 reshape.159
  118.6 2.3 copy.64
  120.9 67.9 %while.15 = (s32[]{:T(128)}, f32[1792,128]{1,0:T(8,128)S(1)}, f32[1792,128]{1,0:T(8,128)}, f32[6,2,256,128]{3,2,1,0:T(8,128)}, pred[256,1792]{1,0:T(8,128)(4,1)S...) while((s32[]{:T(128)}, f32[1792,128]{1,0:T(8,128)S(1)}, ...), condition=%wide.region_9.10_spmd.clone, body=%wide.region_5.9_spmd.clone.sunk | while | flops 1188461568 | bytes 80503144 | solution.py:174
  120.9 2.0 fusion.73
  125.5 1.4 fusion.76
  126.9 2.1 fusion.74
  129.0 2.9 %fusion.75 = f32[1792,128]{1,0:T(8,128)} fusion(f32[2,256,1792]{2,1,0:T(8,128)S(1)} %copy-done.2, f32[2,256]{1,0:T(2,128)S(1)} %log_add_fusion.2, f32[1792,128]{1,0:T(8,128)} %get-tuple-element.220, pred[]{:T(512)S(6)} %compare.30, bf16[6,2,256,128]{3,2,1,0:T(8,128)(2,1)} %copy-done.8, s32[]{:T(128)} %get-tuple-element.218), kind=kOutput, calls=%fused_computation.11.clone.1 | convolution fusion | flops 237174784 | bytes 5638657 | tf_op jit(solution)/shard_map/while/body/eval_jaxpr/htk,htd->kd/dot_general | solution.py:168
  132.0 2.0 fusion.73
  136.6 1.4 fusion.76
  137.9 2.1 fusion.74
  140.0 3.3 %fusion.75 = f32[1792,128]{1,0:T(8,128)} fusion(f32[2,256,1792]{2,1,0:T(8,128)S(1)} %copy-done.2, f32[2,256]{1,0:T(2,128)S(1)} %log_add_fusion.2, f32[1792,128]{1,0:T(8,128)} %get-tuple-element.220, pred[]{:T(512)S(6)} %compare.30, bf16[6,2,256,128]{3,2,1,0:T(8,128)(2,1)} %copy-done.8, s32[]{:T(128)} %get-tuple-element.218), kind=kOutput, calls=%fused_computation.11.clone.1 | convolution fusion | flops 237174784 | bytes 5638657 | tf_op jit(solution)/shard_map/while/body/eval_jaxpr/htk,htd->kd/dot_general | solution.py:168
  143.4 2.0 fusion.73
  147.9 1.4 fusion.76
  149.3 2.1 fusion.74
  151.4 3.3 %fusion.75 = f32[1792,128]{1,0:T(8,128)} fusion(f32[2,256,1792]{2,1,0:T(8,128)S(1)} %copy-done.2, f32[2,256]{1,0:T(2,128)S(1)} %log_add_fusion.2, f32[1792,128]{1,0:T(8,128)} %get-tuple-element.220, pred[]{:T(512)S(6)} %compare.30, bf16[6,2,256,128]{3,2,1,0:T(8,128)(2,1)} %copy-done.8, s32[]{:T(128)} %get-tuple-element.218), kind=kOutput, calls=%fused_computation.11.clone.1 | convolution fusion | flops 237174784 | bytes 5638657 | tf_op jit(solution)/shard_map/while/body/eval_jaxpr/htk,htd->kd/dot_general | solution.py:168
  154.7 2.0 fusion.73
  159.3 1.4 fusion.76
  160.7 2.1 fusion.74
  162.8 3.3 %fusion.75 = f32[1792,128]{1,0:T(8,128)} fusion(f32[2,256,1792]{2,1,0:T(8,128)S(1)} %copy-done.2, f32[2,256]{1,0:T(2,128)S(1)} %log_add_fusion.2, f32[1792,128]{1,0:T(8,128)} %get-tuple-element.220, pred[]{:T(512)S(6)} %compare.30, bf16[6,2,256,128]{3,2,1,0:T(8,128)(2,1)} %copy-done.8, s32[]{:T(128)} %get-tuple-element.218), kind=kOutput, calls=%fused_computation.11.clone.1 | convolution fusion | flops 237174784 | bytes 5638657 | tf_op jit(solution)/shard_map/while/body/eval_jaxpr/htk,htd->kd/dot_general | solution.py:168
  166.1 2.0 fusion.73
  170.7 1.4 fusion.76
  172.1 2.1 fusion.74
  174.2 3.3 %fusion.75 = f32[1792,128]{1,0:T(8,128)} fusion(f32[2,256,1792]{2,1,0:T(8,128)S(1)} %copy-done.2, f32[2,256]{1,0:T(2,128)S(1)} %log_add_fusion.2, f32[1792,128]{1,0:T(8,128)} %get-tuple-element.220, pred[]{:T(512)S(6)} %compare.30, bf16[6,2,256,128]{3,2,1,0:T(8,128)(2,1)} %copy-done.8, s32[]{:T(128)} %get-tuple-element.218), kind=kOutput, calls=%fused_computation.11.clone.1 | convolution fusion | flops 237174784 | bytes 5638657 | tf_op jit(solution)/shard_map/while/body/eval_jaxpr/htk,htd->kd/dot_general | solution.py:168
  177.5 2.0 fusion.73
  182.1 1.4 fusion.76
  183.5 2.1 fusion.74
  185.6 3.3 %fusion.75 = f32[1792,128]{1,0:T(8,128)} fusion(f32[2,256,1792]{2,1,0:T(8,128)S(1)} %copy-done.2, f32[2,256]{1,0:T(2,128)S(1)} %log_add_fusion.2, f32[1792,128]{1,0:T(8,128)} %get-tuple-element.220, pred[]{:T(512)S(6)} %compare.30, bf16[6,2,256,128]{3,2,1,0:T(8,128)(2,1)} %copy-done.8, s32[]{:T(128)} %get-tuple-element.218), kind=kOutput, calls=%fused_computation.11.clone.1 | convolution fusion | flops 237174784 | bytes 5638657 | tf_op jit(solution)/shard_map/while/body/eval_jaxpr/htk,htd->kd/dot_general | solution.py:168
  189.0 1.1 copy-done.3
  192.0 1.3 collective-permute-start.11
  193.2 1.3 collective-permute-start.12
  194.5 1.3 collective-permute-start.13
  195.8 1.5 collective-permute-start.14
  197.3 2.4 copy.94
  199.7 1.4 all_to_all.108
  201.1 3.6 %all-to-all-start.4 = ((f32[4,64,1536]{2,1,0:T(8,128)}), f32[4,64,1536]{2,1,0:T(8,128)S(1)}, u32[]{:S(2)}, u32[]{:S(2)}) async-start(f32[4,64,1536]{2,1,0:T(8,128)} %all_to_all.108), calls=%async_computation.4 | async-start | bytes 3145728 | tf_op jit(solution)/shard_map/all_to_all | solution.py:200
  204.6 50.2 %all-reduce.1 = s32[64]{0:T(128)S(1)} all-reduce(s32[64]{0:T(128)S(1)} %get-tuple-element.118), channel_id=1, replica_groups=mesh['ctx'=8,'head'=4] {'ctx'}, use_global_device_ids=true, to_apply=%add.1 | all-reduce | flops 64 | bytes 512
  254.9 1.2 fusion.28
  256.1 2.8 fusion.24
  260.2 3.3 %all-to-all-start.6 = ((f32[4,64,128]{2,1,0:T(8,128)}), f32[4,64,128]{2,1,0:T(8,128)S(1)}, u32[]{:S(2)}, u32[]{:S(2)}) async-start(f32[4,64,128]{2,1,0:T(8,128)} %bitcast.39), calls=%async_computation.6 | async-start | bytes 262144 | tf_op jit(solution)/shard_map/all_to_all | solution.py:202
  263.6 1.3 copy.81
  264.9 3.3 %all-to-all-done.6 = f32[4,64,128]{2,1,0:T(8,128)S(1)} async-done(((f32[4,64,128]{2,1,0:T(8,128)}), f32[4,64,128]{2,1,0:T(8,128)S(1)}, u32[]{:S(2)}, u32[]{:S(2)}) %all-to-all-start.6) | async-done | bytes 131104 | tf_op jit(solution)/shard_map/all_to_all | solution.py:202
  268.1 3.3 %all-to-all-start.5 = ((f32[4,64,128]{2,1,0:T(8,128)}), f32[4,64,128]{2,1,0:T(8,128)S(1)}, u32[]{:S(2)}, u32[]{:S(2)}) async-start(f32[4,64,128]{2,1,0:T(8,128)} %bitcast.37), calls=%async_computation.5 | async-start | bytes 262144 | tf_op jit(solution)/shard_map/all_to_all | solution.py:201
  272.1 3.9 %all-to-all-done.5 = f32[4,64,128]{2,1,0:T(8,128)S(1)} async-done(((f32[4,64,128]{2,1,0:T(8,128)}), f32[4,64,128]{2,1,0:T(8,128)S(1)}, u32[]{:S(2)}, u32[]{:S(2)}) %all-to-all-start.5) | async-done | bytes 131104 | tf_op jit(solution)/shard_map/all_to_all | solution.py:201
  (214 shorter events, 39.5 us)
Async XLA Ops:
  7.2 26.8 %copy-start.11 = (bf16[64,6144]{1,0:T(8,128)(2,1)S(1)}, bf16[64,6144]{1,0:T(8,128)(2,1)}, u32[]{:S(2)}) copy-start(bf16[64,6144]{1,0:T(8,128)(2,1)} %param.12) | copy-start | bytes 2359300
  8.7 19.4 %all-to-all-start.1 = ((bf16[64,4,128]{2,0,1:T(8,128)(2,1)}), bf16[64,4,128]{2,0,1:T(8,128)(2,1)S(1)}, u32[]{:S(2)}, u32[]{:S(2)}) async-start(bf16[64,4,128]{2,0,1:T(8,128)(2,1)} %copy_bitcast_fusion.6), calls=%async_computation.1 | async-start | bytes 131072 | tf_op jit(solution)/shard_map/all_to_all | solution.py:85
  28.1 7.6 %all-to-all-start.2 = ((bf16[64,4,128]{2,0,1:T(8,128)(2,1)}), bf16[64,4,128]{2,0,1:T(8,128)(2,1)S(1)}, u32[]{:S(2)}, u32[]{:S(2)}) async-start(bf16[64,4,128]{2,0,1:T(8,128)(2,1)} %copy_bitcast_fusion.5), calls=%async_computation.2 | async-start | bytes 131072 | tf_op jit(solution)/shard_map/all_to_all | solution.py:86
  35.6 64.7 %all-to-all-start.3 = ((bf16[64,4,1536]{2,0,1:T(8,128)(2,1)}), bf16[64,4,1536]{2,0,1:T(8,128)(2,1)S(1)}, u32[]{:S(2)}, u32[]{:S(2)}) async-start(bf16[64,4,1536]{2,0,1:T(8,128)(2,1)} %bitcast.127), calls=%async_computation.3 | async-start | bytes 1572864 | tf_op jit(solution)/shard_map/all_to_all | solution.py:87
  39.2 8.1 %collective-permute-start.4 = (bf16[64,256]{1,0:T(8,128)(2,1)S(1)}, bf16[64,256]{1,0:T(8,128)(2,1)S(1)}, u32[]{:S(2)}, u32[]{:S(2)}) collective-permute-start(bf16[64,256]{1,0:T(8,128)(2,1)S(1)} %fusion.29), channel_id=1, source_target_pairs={{0,4},{4,8},{8,12},{12,16},{16,20},{20,24},{24,28},{28,0},{1,5},{5... | collective-permute-start | bytes 98312 | tf_op jit(solution)/shard_map/ppermute | solution.py:24
  41.3 9.6 %collective-permute-start.8 = (bf16[64,256]{1,0:T(8,128)(2,1)S(1)}, bf16[64,256]{1,0:T(8,128)(2,1)S(1)}, u32[]{:S(2)}, u32[]{:S(2)}) collective-permute-start(bf16[64,256]{1,0:T(8,128)(2,1)S(1)} %fusion.29), channel_id=1, source_target_pairs={{4,0},{8,4},{12,8},{16,12},{20,16},{24,20},{28,24},{0,28},{5,1},{9... | collective-permute-start | bytes 98312 | tf_op jit(solution)/shard_map/ppermute | solution.py:26
  44.4 44.2 %collective-permute-start = (bf16[256,256]{1,0:T(8,128)(2,1)S(1)}, bf16[256,256]{1,0:T(8,128)(2,1)S(1)}, u32[]{:S(2)}, u32[]{:S(2)}) collective-permute-start(bf16[256,256]{1,0:T(8,128)(2,1)S(1)} %pad_maximum_fusion), channel_id=1, source_target_pairs={{0,16},{4,20},{8,24},{12,28},{1,17},{5,21},{9,25},{13,29},{2,18},{... | collective-permute-start | bytes 393224 | tf_op jit(solution)/shard_map/ppermute | solution.py:36
  47.2 6.7 %collective-permute-start.5 = (bf16[64,256]{1,0:T(8,128)(2,1)S(1)}, bf16[64,256]{1,0:T(8,128)(2,1)S(1)}, u32[]{:S(2)}, u32[]{:S(2)}) collective-permute-start(bf16[64,256]{1,0:T(8,128)(2,1)S(1)} %collective-permute-done.4), channel_id=1, source_target_pairs={{0,4},{4,8},{8,12},{12,16},{16,20},{20,24},{24,28},{28,0},{1,5},{5... | collective-permute-start | bytes 98312 | tf_op jit(solution)/shard_map/ppermute | solution.py:24
  47.9 43.4 %collective-permute-start.1 = (bf16[256,256]{1,0:T(8,128)(2,1)S(1)}, bf16[256,256]{1,0:T(8,128)(2,1)S(1)}, u32[]{:S(2)}, u32[]{:S(2)}) collective-permute-start(bf16[256,256]{1,0:T(8,128)(2,1)S(1)} %pad_maximum_fusion), channel_id=1, source_target_pairs={{0,12},{4,16},{8,20},{12,24},{16,28},{1,13},{5,17},{9,21},{13,25},... | collective-permute-start | bytes 393224 | tf_op jit(solution)/shard_map/ppermute | solution.py:36
  50.9 32.4 %collective-permute-start.9 = (bf16[64,256]{1,0:T(8,128)(2,1)S(1)}, bf16[64,256]{1,0:T(8,128)(2,1)S(1)}, u32[]{:S(2)}, u32[]{:S(2)}) collective-permute-start(bf16[64,256]{1,0:T(8,128)(2,1)S(1)} %collective-permute-done.8), channel_id=1, source_target_pairs={{4,0},{8,4},{12,8},{16,12},{20,16},{24,20},{28,24},{0,28},{5,1},{9... | collective-permute-start | bytes 98312 | tf_op jit(solution)/shard_map/ppermute | solution.py:26
  53.9 34.7 %collective-permute-start.6 = (bf16[64,256]{1,0:T(8,128)(2,1)S(1)}, bf16[64,256]{1,0:T(8,128)(2,1)S(1)}, u32[]{:S(2)}, u32[]{:S(2)}) collective-permute-start(bf16[64,256]{1,0:T(8,128)(2,1)S(1)} %collective-permute-done.5), channel_id=1, source_target_pairs={{0,4},{4,8},{8,12},{12,16},{16,20},{20,24},{24,28},{28,0},{1,5},{5... | collective-permute-start | bytes 98312 | tf_op jit(solution)/shard_map/ppermute | solution.py:24
  76.8 15.2 %collective-permute-start.2 = (bf16[256,256]{1,0:T(8,128)(2,1)S(1)}, bf16[256,256]{1,0:T(8,128)(2,1)S(1)}, u32[]{:S(2)}, u32[]{:S(2)}) collective-permute-start(bf16[256,256]{1,0:T(8,128)(2,1)S(1)} %pad_maximum_fusion), channel_id=1, source_target_pairs={{0,8},{4,12},{8,16},{12,20},{16,24},{20,28},{1,9},{5,13},{9,17},{1... | collective-permute-start | bytes 393224 | tf_op jit(solution)/shard_map/ppermute | solution.py:36
  83.3 9.4 %collective-permute-start.3 = (bf16[256,256]{1,0:T(8,128)(2,1)S(1)}, bf16[256,256]{1,0:T(8,128)(2,1)S(1)}, u32[]{:S(2)}, u32[]{:S(2)}) collective-permute-start(bf16[256,256]{1,0:T(8,128)(2,1)S(1)} %pad_maximum_fusion), channel_id=1, source_target_pairs={{0,4},{4,8},{8,12},{12,16},{16,20},{20,24},{24,28},{1,5},{5,9},{9,... | collective-permute-start | bytes 393224 | tf_op jit(solution)/shard_map/ppermute | solution.py:36
  88.6 6.8 %collective-permute-start.10 = (bf16[64,256]{1,0:T(8,128)(2,1)S(1)}, bf16[64,256]{1,0:T(8,128)(2,1)S(1)}, u32[]{:S(2)}, u32[]{:S(2)}) collective-permute-start(bf16[64,256]{1,0:T(8,128)(2,1)S(1)} %collective-permute-done.9), channel_id=1, source_target_pairs={{4,0},{8,4},{12,8},{16,12},{20,16},{24,20},{28,24},{0,28},{5,1},{9... | collective-permute-start | bytes 98312 | tf_op jit(solution)/shard_map/ppermute | solution.py:26
  88.7 6.7 %collective-permute-start.7 = (bf16[64,256]{1,0:T(8,128)(2,1)S(1)}, bf16[64,256]{1,0:T(8,128)(2,1)S(1)}, u32[]{:S(2)}, u32[]{:S(2)}) collective-permute-start(bf16[64,256]{1,0:T(8,128)(2,1)S(1)} %collective-permute-done.6), channel_id=1, source_target_pairs={{0,4},{4,8},{8,12},{12,16},{16,20},{20,24},{24,28},{28,0},{1,5},{5... | collective-permute-start | bytes 98312 | tf_op jit(solution)/shard_map/ppermute | solution.py:24
  100.3 15.9 %all-to-all-start = ((bf16[64,4,1536]{2,0,1:T(8,128)(2,1)}), bf16[64,4,1536]{2,0,1:T(8,128)(2,1)}, u32[]{:S(2)}, u32[]{:S(2)}) async-start(bf16[64,4,1536]{2,0,1:T(8,128)(2,1)} %bitcast.160), calls=%async_computation | async-start | bytes 1572864 | tf_op jit(solution)/shard_map/all_to_all | solution.py:84
  104.5 151.6 %all-gather.2.cloned.1.call-start = ((), (), s32[]{:S(2)}) async-start(), calls=%async_computation.7 | async-start | bytes 2359296 | tf_op jit(solution)/shard_map/all_gather | solution.py:193
  120.9 2.6 copy-start.6
  120.9 3.6 %copy-start.8 = (bf16[6,2,256,128]{3,2,1,0:T(8,128)(2,1)}, bf16[6,2,256,128]{3,2,1,0:T(8,128)(2,1)S(1)}, u32[]{:S(2)}) copy-start(bf16[6,2,256,128]{3,2,1,0:T(8,128)(2,1)S(1)} %get-tuple-element.236) | copy-start | bytes 2359300 | tf_op jit(solution)/shard_map/while
  126.9 2.1 copy-start.2
  129.0 3.0 %copy-start.5 = (pred[256,1792]{1,0:T(8,128)(4,1)S(1)}, pred[256,1792]{1,0:T(8,128)(4,1)}, u32[]{:S(2)}) copy-start(pred[256,1792]{1,0:T(8,128)(4,1)} %copy-done.4) | copy-start | bytes 1376260 | tf_op jit(solution)/shard_map/while
  129.0 3.0 %copy-start.7 = (bf16[1792,128]{1,0:T(8,128)(2,1)S(1)}, bf16[1792,128]{1,0:T(8,128)(2,1)}, u32[]{:S(2)}) copy-start(bf16[1792,128]{1,0:T(8,128)(2,1)} %copy-done.6) | copy-start | bytes 1376260 | tf_op jit(solution)/shard_map/while
  129.0 2.9 %copy-start.9 = (bf16[6,2,256,128]{3,2,1,0:T(8,128)(2,1)S(1)}, bf16[6,2,256,128]{3,2,1,0:T(8,128)(2,1)}, u32[]{:S(2)}) copy-start(bf16[6,2,256,128]{3,2,1,0:T(8,128)(2,1)} %copy-done.8) | copy-start | bytes 2359300 | tf_op jit(solution)/shard_map/while
  131.9 2.7 copy-start.6
  132.0 3.6 %copy-start.8 = (bf16[6,2,256,128]{3,2,1,0:T(8,128)(2,1)}, bf16[6,2,256,128]{3,2,1,0:T(8,128)(2,1)S(1)}, u32[]{:S(2)}) copy-start(bf16[6,2,256,128]{3,2,1,0:T(8,128)(2,1)S(1)} %get-tuple-element.236) | copy-start | bytes 2359300 | tf_op jit(solution)/shard_map/while
  137.9 2.1 copy-start.2
  140.0 3.3 %copy-start.5 = (pred[256,1792]{1,0:T(8,128)(4,1)S(1)}, pred[256,1792]{1,0:T(8,128)(4,1)}, u32[]{:S(2)}) copy-start(pred[256,1792]{1,0:T(8,128)(4,1)} %copy-done.4) | copy-start | bytes 1376260 | tf_op jit(solution)/shard_map/while
  140.0 3.3 %copy-start.7 = (bf16[1792,128]{1,0:T(8,128)(2,1)S(1)}, bf16[1792,128]{1,0:T(8,128)(2,1)}, u32[]{:S(2)}) copy-start(bf16[1792,128]{1,0:T(8,128)(2,1)} %copy-done.6) | copy-start | bytes 1376260 | tf_op jit(solution)/shard_map/while
  140.0 3.3 %copy-start.9 = (bf16[6,2,256,128]{3,2,1,0:T(8,128)(2,1)S(1)}, bf16[6,2,256,128]{3,2,1,0:T(8,128)(2,1)}, u32[]{:S(2)}) copy-start(bf16[6,2,256,128]{3,2,1,0:T(8,128)(2,1)} %copy-done.8) | copy-start | bytes 2359300 | tf_op jit(solution)/shard_map/while
  143.3 2.7 copy-start.6
  143.3 3.6 %copy-start.8 = (bf16[6,2,256,128]{3,2,1,0:T(8,128)(2,1)}, bf16[6,2,256,128]{3,2,1,0:T(8,128)(2,1)S(1)}, u32[]{:S(2)}) copy-start(bf16[6,2,256,128]{3,2,1,0:T(8,128)(2,1)S(1)} %get-tuple-element.236) | copy-start | bytes 2359300 | tf_op jit(solution)/shard_map/while
  149.3 2.1 copy-start.2
  151.4 3.3 %copy-start.5 = (pred[256,1792]{1,0:T(8,128)(4,1)S(1)}, pred[256,1792]{1,0:T(8,128)(4,1)}, u32[]{:S(2)}) copy-start(pred[256,1792]{1,0:T(8,128)(4,1)} %copy-done.4) | copy-start | bytes 1376260 | tf_op jit(solution)/shard_map/while
  151.4 3.3 %copy-start.7 = (bf16[1792,128]{1,0:T(8,128)(2,1)S(1)}, bf16[1792,128]{1,0:T(8,128)(2,1)}, u32[]{:S(2)}) copy-start(bf16[1792,128]{1,0:T(8,128)(2,1)} %copy-done.6) | copy-start | bytes 1376260 | tf_op jit(solution)/shard_map/while
  151.4 3.3 %copy-start.9 = (bf16[6,2,256,128]{3,2,1,0:T(8,128)(2,1)S(1)}, bf16[6,2,256,128]{3,2,1,0:T(8,128)(2,1)}, u32[]{:S(2)}) copy-start(bf16[6,2,256,128]{3,2,1,0:T(8,128)(2,1)} %copy-done.8) | copy-start | bytes 2359300 | tf_op jit(solution)/shard_map/while
  154.7 2.0 copy-start.4
  154.7 2.7 copy-start.6
  154.7 3.6 %copy-start.8 = (bf16[6,2,256,128]{3,2,1,0:T(8,128)(2,1)}, bf16[6,2,256,128]{3,2,1,0:T(8,128)(2,1)S(1)}, u32[]{:S(2)}) copy-start(bf16[6,2,256,128]{3,2,1,0:T(8,128)(2,1)S(1)} %get-tuple-element.236) | copy-start | bytes 2359300 | tf_op jit(solution)/shard_map/while
  160.7 2.1 copy-start.2
  162.8 3.3 %copy-start.5 = (pred[256,1792]{1,0:T(8,128)(4,1)S(1)}, pred[256,1792]{1,0:T(8,128)(4,1)}, u32[]{:S(2)}) copy-start(pred[256,1792]{1,0:T(8,128)(4,1)} %copy-done.4) | copy-start | bytes 1376260 | tf_op jit(solution)/shard_map/while
  162.8 3.3 %copy-start.7 = (bf16[1792,128]{1,0:T(8,128)(2,1)S(1)}, bf16[1792,128]{1,0:T(8,128)(2,1)}, u32[]{:S(2)}) copy-start(bf16[1792,128]{1,0:T(8,128)(2,1)} %copy-done.6) | copy-start | bytes 1376260 | tf_op jit(solution)/shard_map/while
  162.8 3.3 %copy-start.9 = (bf16[6,2,256,128]{3,2,1,0:T(8,128)(2,1)S(1)}, bf16[6,2,256,128]{3,2,1,0:T(8,128)(2,1)}, u32[]{:S(2)}) copy-start(bf16[6,2,256,128]{3,2,1,0:T(8,128)(2,1)} %copy-done.8) | copy-start | bytes 2359300 | tf_op jit(solution)/shard_map/while
  166.1 2.0 copy-start.4
  166.1 2.7 copy-start.6
  166.1 3.6 %copy-start.8 = (bf16[6,2,256,128]{3,2,1,0:T(8,128)(2,1)}, bf16[6,2,256,128]{3,2,1,0:T(8,128)(2,1)S(1)}, u32[]{:S(2)}) copy-start(bf16[6,2,256,128]{3,2,1,0:T(8,128)(2,1)S(1)} %get-tuple-element.236) | copy-start | bytes 2359300 | tf_op jit(solution)/shard_map/while
  172.1 2.1 copy-start.2
  174.2 3.3 %copy-start.5 = (pred[256,1792]{1,0:T(8,128)(4,1)S(1)}, pred[256,1792]{1,0:T(8,128)(4,1)}, u32[]{:S(2)}) copy-start(pred[256,1792]{1,0:T(8,128)(4,1)} %copy-done.4) | copy-start | bytes 1376260 | tf_op jit(solution)/shard_map/while
  174.2 3.3 %copy-start.7 = (bf16[1792,128]{1,0:T(8,128)(2,1)S(1)}, bf16[1792,128]{1,0:T(8,128)(2,1)}, u32[]{:S(2)}) copy-start(bf16[1792,128]{1,0:T(8,128)(2,1)} %copy-done.6) | copy-start | bytes 1376260 | tf_op jit(solution)/shard_map/while
  174.2 3.3 %copy-start.9 = (bf16[6,2,256,128]{3,2,1,0:T(8,128)(2,1)S(1)}, bf16[6,2,256,128]{3,2,1,0:T(8,128)(2,1)}, u32[]{:S(2)}) copy-start(bf16[6,2,256,128]{3,2,1,0:T(8,128)(2,1)} %copy-done.8) | copy-start | bytes 2359300 | tf_op jit(solution)/shard_map/while
  177.5 2.0 copy-start.4
  177.5 2.7 copy-start.6
  177.5 3.6 %copy-start.8 = (bf16[6,2,256,128]{3,2,1,0:T(8,128)(2,1)}, bf16[6,2,256,128]{3,2,1,0:T(8,128)(2,1)S(1)}, u32[]{:S(2)}) copy-start(bf16[6,2,256,128]{3,2,1,0:T(8,128)(2,1)S(1)} %get-tuple-element.236) | copy-start | bytes 2359300 | tf_op jit(solution)/shard_map/while
  183.5 2.1 copy-start.2
  185.6 3.3 %copy-start.5 = (pred[256,1792]{1,0:T(8,128)(4,1)S(1)}, pred[256,1792]{1,0:T(8,128)(4,1)}, u32[]{:S(2)}) copy-start(pred[256,1792]{1,0:T(8,128)(4,1)} %copy-done.4) | copy-start | bytes 1376260 | tf_op jit(solution)/shard_map/while
  185.6 3.3 %copy-start.7 = (bf16[1792,128]{1,0:T(8,128)(2,1)S(1)}, bf16[1792,128]{1,0:T(8,128)(2,1)}, u32[]{:S(2)}) copy-start(bf16[1792,128]{1,0:T(8,128)(2,1)} %copy-done.6) | copy-start | bytes 1376260 | tf_op jit(solution)/shard_map/while
  185.6 3.3 %copy-start.9 = (bf16[6,2,256,128]{3,2,1,0:T(8,128)(2,1)S(1)}, bf16[6,2,256,128]{3,2,1,0:T(8,128)(2,1)}, u32[]{:S(2)}) copy-start(bf16[6,2,256,128]{3,2,1,0:T(8,128)(2,1)} %copy-done.8) | copy-start | bytes 2359300 | tf_op jit(solution)/shard_map/while
  190.1 7.2 %copy-start.10 = (f32[1792,256]{1,0:T(8,128)}, f32[1792,256]{1,0:T(8,128)S(1)}, u32[]{:S(2)}) copy-start(f32[1792,256]{1,0:T(8,128)S(1)} %constant_dynamic-update-slice_fusion.21) | copy-start | bytes 5505028
  192.0 62.9 %collective-permute-start.11 = (f32[256,256]{1,0:T(8,128)}, f32[256,256]{1,0:T(8,128)S(1)}, u32[]{:S(2)}, u32[]{:S(2)}) collective-permute-start(f32[256,256]{1,0:T(8,128)} %get-tuple-element.124), channel_id=1, source_target_pairs={{4,0},{8,4},{12,8},{16,12},{20,16},{24,20},{28,24},{5,1},{9,5},{13... | collective-permute-start | bytes 786440 | tf_op jit(solution)/shard_map/ppermute | solution.py:36
  193.2 61.6 %collective-permute-start.12 = (f32[256,256]{1,0:T(8,128)}, f32[256,256]{1,0:T(8,128)S(1)}, u32[]{:S(2)}, u32[]{:S(2)}) collective-permute-start(f32[256,256]{1,0:T(8,128)} %get-tuple-element.127), channel_id=1, source_target_pairs={{8,0},{12,4},{16,8},{20,12},{24,16},{28,20},{9,1},{13,5},{17,9},{2... | collective-permute-start | bytes 786440 | tf_op jit(solution)/shard_map/ppermute | solution.py:36
  194.5 60.3 %collective-permute-start.13 = (f32[256,256]{1,0:T(8,128)}, f32[256,256]{1,0:T(8,128)}, u32[]{:S(2)}, u32[]{:S(2)}) collective-permute-start(f32[256,256]{1,0:T(8,128)} %get-tuple-element.126), channel_id=1, source_target_pairs={{12,0},{16,4},{20,8},{24,12},{28,16},{13,1},{17,5},{21,9},{25,13},... | collective-permute-start | bytes 786440 | tf_op jit(solution)/shard_map/ppermute | solution.py:36
  195.8 59.0 %collective-permute-start.14 = (f32[256,256]{1,0:T(8,128)}, f32[256,256]{1,0:T(8,128)}, u32[]{:S(2)}, u32[]{:S(2)}) collective-permute-start(f32[256,256]{1,0:T(8,128)} %get-tuple-element.125), channel_id=1, source_target_pairs={{16,0},{20,4},{24,8},{28,12},{17,1},{21,5},{25,9},{29,13},{18,2},{... | collective-permute-start | bytes 786440 | tf_op jit(solution)/shard_map/ppermute | solution.py:36
  201.1 59.2 %all-to-all-start.4 = ((f32[4,64,1536]{2,1,0:T(8,128)}), f32[4,64,1536]{2,1,0:T(8,128)S(1)}, u32[]{:S(2)}, u32[]{:S(2)}) async-start(f32[4,64,1536]{2,1,0:T(8,128)} %all_to_all.108), calls=%async_computation.4 | async-start | bytes 3145728 | tf_op jit(solution)/shard_map/all_to_all | solution.py:200
  260.2 7.9 %all-to-all-start.6 = ((f32[4,64,128]{2,1,0:T(8,128)}), f32[4,64,128]{2,1,0:T(8,128)S(1)}, u32[]{:S(2)}, u32[]{:S(2)}) async-start(f32[4,64,128]{2,1,0:T(8,128)} %bitcast.39), calls=%async_computation.6 | async-start | bytes 262144 | tf_op jit(solution)/shard_map/all_to_all | solution.py:202
  268.1 7.9 %all-to-all-start.5 = ((f32[4,64,128]{2,1,0:T(8,128)}), f32[4,64,128]{2,1,0:T(8,128)S(1)}, u32[]{:S(2)}, u32[]{:S(2)}) async-start(f32[4,64,128]{2,1,0:T(8,128)} %bitcast.37), calls=%async_computation.5 | async-start | bytes 262144 | tf_op jit(solution)/shard_map/all_to_all | solution.py:201
  (11 other events, 18.7 us)
Sparse Core Ops, SparseCore 0:
  191.1 64.2 all-gather.1
